TPU v7x, 32 devices: a whole 2x2x4 slice. The times are simulated.
32 devices in a mesh: groups: 2 (over y), ctx: 4 (over x, core), chan: 4 (over z).
Axes of the slice: x: 2, y: 2, z: 4, core: 2. Of those that a mesh axis runs over, the one named last changes fastest.
Arguments:
- stream: bfloat16 [1536, 4096], P(('groups', 'ctx'), 'chan'), parts along dimension 0, may hold values from -30 to 30
- in_weights: bfloat16 [2, 4096, 3, 2048], P(None, 'ctx', None, 'chan'), may hold values from -0.09375 to 0.09375
- out_weights: bfloat16 [2, 4096, 2048], P(None, 'ctx', 'chan'), may hold values from -0.125 to 0.125
- short_taps: bfloat16 [7, 2048], P(None, 'chan'), may hold values from -2.390625 to 2.390625
- medium_taps: bfloat16 [128, 128], P(None, 'chan'), may hold values from -0.5390625 to 0.5390625
- plan: int32 [4], replicated, may hold values from 0 to 1
Outputs:
- result: bfloat16 [1536, 4096], P(('groups', 'ctx'), 'chan'), parts along dimension 0
There are 2 independent parts, one for each index of `groups`. A program takes and returns all parts, laid end to end along the dimension named above; an argument that names none is the same for every part. Nothing has to cross between parts.
All inputs are finite; a program needn't handle non-finite values.
Results may differ from a plain program's by a relative error of at most 0.03.
Values may be sent and summed in bfloat16 or wider, within the bound.
A program may use at most 128 MiB of HBM per device.

v0:
```python
from functools import partial

import jax
import jax.numpy as jnp
from jax import lax
from jax.sharding import PartitionSpec as P

STEPS = 4


def passed_along(value, axis, steps):
    count = lax.axis_size(axis)
    leading, last = (max(0, -steps), min(count, count - steps))
    return lax.ppermute(value, axis, [(source, source + steps) for source in range(leading, last)])


def section_taps(section, short_taps, medium_taps):
    reach = medium_taps.shape[0]
    channels = short_taps.shape[1]
    padding = jnp.zeros((reach - short_taps.shape[0], channels), short_taps.dtype)
    short_full = jnp.concatenate([short_taps, padding], 0)
    group_size = channels // medium_taps.shape[1]
    medium_full = jnp.broadcast_to(
        medium_taps[:, :, None], (reach, medium_taps.shape[1], group_size)
    ).reshape(reach, channels)
    return jnp.where(section == 0, short_full, medium_full)


def causal_filter(extended, filter_taps):
    filtered = lax.conv_general_dilated(
        extended[None],
        filter_taps[::-1][:, None, :],
        (1,),
        "VALID",
        dimension_numbers=("NWC", "WIO", "NWC"),
        feature_group_count=filter_taps.shape[1],
        preferred_element_type=jnp.float32,
    )
    return filtered[0]


def filter_gate(projected, section, short_taps, medium_taps):
    query_bf = projected[:, 0].astype(jnp.bfloat16)
    mixed_bf = (projected[:, 1] * projected[:, 2]).astype(jnp.bfloat16)
    reach = medium_taps.shape[0]
    earlier = passed_along(mixed_bf[-reach:], "ctx", 1)
    extended = jnp.concatenate([earlier[1:], mixed_bf], 0)
    filtered = causal_filter(extended, section_taps(section, short_taps, medium_taps))
    return (query_bf.astype(jnp.float32) * filtered).astype(jnp.bfloat16)


def expand_rows(hidden):
    return lax.all_gather(hidden, "chan", axis=1, tiled=True)


def combine(hidden, partial_sum):
    update = lax.psum_scatter(
        partial_sum.astype(jnp.bfloat16), "chan", scatter_dimension=1, tiled=True
    ).astype(jnp.float32)
    return (hidden.astype(jnp.float32) + update).astype(jnp.bfloat16)


def advance(hidden, section, project, emit, short_taps, medium_taps):
    full_rows = expand_rows(hidden)
    widened = full_rows.astype(jnp.float32)
    row_scale = lax.rsqrt(jnp.mean(widened * widened, axis=1, keepdims=True) + 1e-05)
    projected, kept_in = project(full_rows, section)
    projected = projected.reshape(full_rows.shape[0], 3, -1) * row_scale[:, :, None]
    gated_bf = filter_gate(projected, section, short_taps, medium_taps)
    partial_sum, kept_out = emit(gated_bf, section)
    return (combine(hidden, partial_sum), kept_in, kept_out)


def stored_project(weights_in, full_rows, section):
    chosen = lax.dynamic_index_in_dim(weights_in, section, 0, keepdims=False)
    projected = jnp.dot(
        full_rows, chosen.reshape(chosen.shape[0], -1), preferred_element_type=jnp.float32
    )
    return (projected, weights_in)


def stored_emit(weights_out, gated_bf, section):
    chosen = lax.dynamic_index_in_dim(weights_out, section, 0, keepdims=False)
    product = lax.dot_general(
        gated_bf, chosen, (((1,), (1,)), ((), ())), preferred_element_type=jnp.float32
    )
    return (product, weights_out)


def shards(stream, in_weights, out_weights, short_taps, medium_taps, plan):
    hidden = stream
    weights_in, weights_out = (
        lax.all_gather(in_weights, "ctx", axis=1, tiled=True),
        lax.all_gather(out_weights, "ctx", axis=1, tiled=True),
    )
    first_step = 0
    for step_index in range(first_step, STEPS):
        hidden, weights_in, weights_out = advance(
            hidden,
            plan[step_index],
            partial(stored_project, weights_in),
            partial(stored_emit, weights_out),
            short_taps,
            medium_taps,
        )
    return hidden


def solution(mesh):
    return jax.shard_map(
        shards,
        mesh=mesh,
        in_specs=(
            P(("groups", "ctx"), "chan"),
            P(None, "ctx", None, "chan"),
            P(None, "ctx", "chan"),
            P(None, "chan"),
            P(None, "chan"),
            P(),
        ),
        out_specs=P(("groups", "ctx"), "chan"),
        check_vma=False,
    )
```

profile of v0, /device:TPU:0, one launch (start us, length us, event | category | flops | bytes accessed | tf_op | source)
XLA Modules:
  0.0 604.5 jit_solution(14379718234727122975)
XLA Ops:
  7.3 8.6 %copy.34 = bf16[2,1024,3,512]{1,3,2,0:T(8,128)(2,1)} copy(bf16[2,1024,3,512]{3,1,2,0:T(8,128)(2,1)} %param.7) | data formatting | bytes 12582912 | tf_op args[1]
  19.4 29.3 %all-gather.9.cloned.1.call-done = bf16[192,4096]{1,0:T(8,128)(2,1)} async-done(((bf16[192,1024]{1,0:T(8,128)(2,1)}), bf16[192,4096]{1,0:T(8,128)(2,1)}) %all-gather.9.cloned.1.call-update) | async-done | bytes 1572880 | tf_op jit(solution)/shard_map/all_gather | solution.py:53
  50.5 153.4 %all-gather.7.cloned.1.call-done = bf16[2,4096,3,512]{1,3,2,0:T(8,128)(2,1)} async-done(((bf16[2,1024,3,512]{1,3,2,0:T(8,128)(2,1)}), bf16[2,4096,3,512]{1,3,2,0:T(8,128)(2,1)}) %all-gather.7.cloned.1.call-update) | async-done | bytes 25165840 | tf_op jit(solution)/shard_map/all_gather | solution.py:93
  203.9 6.2 %constant_dynamic-slice_fusion = bf16[1,4096,3,512]{1,3,2,0:T(8,128)(2,1)S(1)} fusion(bf16[2,4096,3,512]{1,3,2,0:T(8,128)(2,1)} %all-gather.7.cloned.1.call-done, s32[]{:T(128)S(6)} %select_n.44), kind=kLoop, calls=%fused_computation.94 | loop fusion | bytes 25165828 | tf_op jit(solution)/shard_map/jit(dynamic_index_in_dim)/dynamic_slice | solution.py:75
  210.2 4.3 convolution_bitcast_fusion
  222.6 5.3 fusion.20
  227.9 35.9 %all-gather.11.cloned.1.call-done = bf16[2,4096,512]{2,1,0:T(8,128)(2,1)} async-done(((bf16[2,1024,512]{2,1,0:T(8,128)(2,1)}), bf16[2,4096,512]{2,1,0:T(8,128)(2,1)}) %all-gather.11.cloned.1.call-update) | async-done | bytes 8388624 | tf_op jit(solution)/shard_map/all_gather | solution.py:94
  263.8 4.9 convolution_convert_fusion.3
  268.7 36.9 %reduce-scatter.5.cloned.1.call-done = bf16[192,1024]{1,0:T(8,128)(2,1)} async-done(((bf16[192,4096]{1,0:T(8,128)(2,1)}), bf16[192,1024]{1,0:T(8,128)(2,1)}) %reduce-scatter.5.cloned.1.call-update) | async-done | bytes 393232 | tf_op jit(solution)/shard_map/reduce_scatter | solution.py:57
  310.1 33.5 %all-gather.13.cloned.1.call-done = bf16[192,4096]{1,0:T(8,128)(2,1)} async-done(((bf16[192,1024]{1,0:T(8,128)(2,1)}), bf16[192,4096]{1,0:T(8,128)(2,1)}) %all-gather.13.cloned.1.call-update) | async-done | bytes 1572880 | tf_op jit(solution)/shard_map/all_gather | solution.py:53
  345.6 7.5 %fusion.21 = f32[192,3,512]{2,0,1:T(8,128)S(1)} fusion(bf16[2,4096,3,512]{1,3,2,0:T(8,128)(2,1)} %all-gather.7.cloned.1.call-done, s32[]{:T(128)S(6)} %select_n.47, bf16[192,4096]{1,0:T(8,128)(2,1)S(1)} %copy-done.1, f32[192]{0:T(256)S(1)} %add_rsqrt_fusion.2), kind=kOutput, calls=%fused_computation.31 | convolution fusion | flops 2416214016 | bytes 15336196 | tf_op jit(solution)/shard_map/dot_general | solution.py:76
  355.5 5.6 fusion.40
  361.1 2.7 convolution_convert_fusion.2
  363.9 38.4 %reduce-scatter.7.cloned.1.call-done = bf16[192,1024]{1,0:T(8,128)(2,1)} async-done(((bf16[192,4096]{1,0:T(8,128)(2,1)}), bf16[192,1024]{1,0:T(8,128)(2,1)}) %reduce-scatter.7.cloned.1.call-update) | async-done | bytes 393232 | tf_op jit(solution)/shard_map/reduce_scatter | solution.py:57
  406.9 33.3 %all-gather.15.cloned.1.call-done = bf16[192,4096]{1,0:T(8,128)(2,1)} async-done(((bf16[192,1024]{1,0:T(8,128)(2,1)}), bf16[192,4096]{1,0:T(8,128)(2,1)}) %all-gather.15.cloned.1.call-update) | async-done | bytes 1572880 | tf_op jit(solution)/shard_map/all_gather | solution.py:53
  442.2 7.5 %fusion.26 = f32[192,3,512]{2,0,1:T(8,128)S(1)} fusion(bf16[2,4096,3,512]{1,3,2,0:T(8,128)(2,1)} %all-gather.7.cloned.1.call-done, s32[]{:T(128)S(6)} %select_n.50, bf16[192,4096]{1,0:T(8,128)(2,1)S(1)} %copy-done.2, f32[192]{0:T(256)S(1)} %add_rsqrt_fusion.1), kind=kOutput, calls=%fused_computation.32 | convolution fusion | flops 2416214016 | bytes 15336196 | tf_op jit(solution)/shard_map/dot_general | solution.py:76
  452.1 5.6 fusion.38
  457.7 2.7 convolution_convert_fusion.1
  460.5 38.4 %reduce-scatter.9.cloned.1.call-done = bf16[192,1024]{1,0:T(8,128)(2,1)} async-done(((bf16[192,4096]{1,0:T(8,128)(2,1)}), bf16[192,1024]{1,0:T(8,128)(2,1)}) %reduce-scatter.9.cloned.1.call-update) | async-done | bytes 393232 | tf_op jit(solution)/shard_map/reduce_scatter | solution.py:57
  503.3 33.5 %all-gather.17.cloned.1.call-done = bf16[192,4096]{1,0:T(8,128)(2,1)} async-done(((bf16[192,1024]{1,0:T(8,128)(2,1)}), bf16[192,4096]{1,0:T(8,128)(2,1)}) %all-gather.17.cloned.1.call-update) | async-done | bytes 1572880 | tf_op jit(solution)/shard_map/all_gather | solution.py:53
  538.7 7.4 %fusion.31 = f32[192,3,512]{2,0,1:T(8,128)S(1)} fusion(bf16[2,4096,3,512]{1,3,2,0:T(8,128)(2,1)} %all-gather.7.cloned.1.call-done, s32[]{:T(128)S(6)} %select_n.53, bf16[192,4096]{1,0:T(8,128)(2,1)S(1)} %copy-done, f32[192]{0:T(256)S(1)} %add_rsqrt_fusion), kind=kOutput, calls=%fused_computation.33 | convolution fusion | flops 2416214016 | bytes 15336196 | tf_op jit(solution)/shard_map/dot_general | solution.py:76
  548.9 5.6 fusion.36
  554.5 2.7 convolution_convert_fusion
  557.3 38.5 %reduce-scatter.11.cloned.1.call-done = bf16[192,1024]{1,0:T(8,128)(2,1)} async-done(((bf16[192,4096]{1,0:T(8,128)(2,1)}), bf16[192,1024]{1,0:T(8,128)(2,1)}) %reduce-scatter.11.cloned.1.call-update) | async-done | bytes 393232 | tf_op jit(solution)/shard_map/reduce_scatter | solution.py:57
  (111 shorter events, 32.3 us)
Async XLA Ops:
  6.5 42.1 %all-gather.9.cloned.1.call-start = ((), (), s32[]{:S(2)}) async-start(), calls=%async_computation.5 | async-start | bytes 1966080 | tf_op jit(solution)/shard_map/all_gather | solution.py:53
  7.3 196.7 %all-gather.7.cloned.1.call-start = ((), (), s32[]{:S(2)}) async-start(), calls=%async_computation.4 | async-start | bytes 31457280 | tf_op jit(solution)/shard_map/all_gather | solution.py:93
  16.0 247.8 %all-gather.11.cloned.1.call-start = ((), (), s32[]{:S(2)}) async-start(), calls=%async_computation.6 | async-start | bytes 10485760 | tf_op jit(solution)/shard_map/all_gather | solution.py:94
  16.7 289.0 %reduce-scatter.5.cloned.1.call-start = ((), (), s32[]{:S(2)}) async-start(), calls=%async_computation.7 | async-start | bytes 1966080 | tf_op jit(solution)/shard_map/reduce_scatter | solution.py:57
  50.5 159.7 %copy-start.6 = (bf16[192,4096]{1,0:T(8,128)(2,1)S(1)}, bf16[192,4096]{1,0:T(8,128)(2,1)}, u32[]{:S(2)}) copy-start(bf16[192,4096]{1,0:T(8,128)(2,1)} %all-gather.9.cloned.1.call-done) | copy-start | bytes 4718596
  215.8 5.7 copy-start.8
  215.8 5.9 copy-start.10
  216.8 5.7 collective-permute-start
  268.7 37.0 %copy-start.7 = (bf16[192,1024]{1,0:T(8,128)(2,1)S(1)}, bf16[192,1024]{1,0:T(8,128)(2,1)}, u32[]{:S(2)}) copy-start(bf16[192,1024]{1,0:T(8,128)(2,1)} %param.6) | copy-start | bytes 1179652
  268.7 74.9 %all-gather.13.cloned.1.call-start = ((), (), s32[]{:S(2)}) async-start(), calls=%async_computation.8 | async-start | bytes 1966080 | tf_op jit(solution)/shard_map/all_gather | solution.py:53
  307.6 94.7 %reduce-scatter.7.cloned.1.call-start = ((), (), s32[]{:S(2)}) async-start(), calls=%async_computation.9 | async-start | bytes 1966080 | tf_op jit(solution)/shard_map/reduce_scatter | solution.py:57
  353.1 2.3 collective-permute-start.1
  355.4 5.7 slice-start
  363.8 38.5 %copy-start.5 = (bf16[192,1024]{1,0:T(8,128)(2,1)S(1)}, bf16[192,1024]{1,0:T(8,128)(2,1)}, u32[]{:S(2)}) copy-start(bf16[192,1024]{1,0:T(8,128)(2,1)} %add_convert_fusion.3) | copy-start | bytes 1179652
  363.8 76.4 %all-gather.15.cloned.1.call-start = ((), (), s32[]{:S(2)}) async-start(), calls=%async_computation.10 | async-start | bytes 1966080 | tf_op jit(solution)/shard_map/all_gather | solution.py:53
  404.2 94.7 %reduce-scatter.9.cloned.1.call-start = ((), (), s32[]{:S(2)}) async-start(), calls=%async_computation.11 | async-start | bytes 1966080 | tf_op jit(solution)/shard_map/reduce_scatter | solution.py:57
  449.7 2.3 collective-permute-start.2
  451.0 6.7 %slice-start.2 = ((s8[8388608]{0:T(1024)(128)(4,1)}), s8[4194304]{0:T(1024)(128)(4,1)S(1)}, s32[]{:S(2)}) async-start(s8[8388608]{0:T(1024)(128)(4,1)} %bitcast.141), calls=%async_computation.16 | async-start | bytes 8388608
  460.4 38.5 %copy-start.4 = (bf16[192,1024]{1,0:T(8,128)(2,1)S(1)}, bf16[192,1024]{1,0:T(8,128)(2,1)}, u32[]{:S(2)}) copy-start(bf16[192,1024]{1,0:T(8,128)(2,1)} %add_convert_fusion.2) | copy-start | bytes 1179652
  460.4 76.4 %all-gather.17.cloned.1.call-start = ((), (), s32[]{:S(2)}) async-start(), calls=%async_computation.12 | async-start | bytes 1966080 | tf_op jit(solution)/shard_map/all_gather | solution.py:53
  500.8 95.0 %reduce-scatter.11.cloned.1.call-start = ((), (), s32[]{:S(2)}) async-start(), calls=%async_computation.13 | async-start | bytes 1966080 | tf_op jit(solution)/shard_map/reduce_scatter | solution.py:57
  546.3 8.2 %slice-start.4 = ((s8[8388608]{0:T(1024)(128)(4,1)}), s8[4194304]{0:T(1024)(128)(4,1)S(1)}, s32[]{:S(2)}) async-start(s8[8388608]{0:T(1024)(128)(4,1)} %bitcast.143), calls=%async_computation.18 | async-start | bytes 8388608
  546.3 2.5 collective-permute-start.3
  557.2 38.5 %copy-start.3 = (bf16[192,1024]{1,0:T(8,128)(2,1)S(1)}, bf16[192,1024]{1,0:T(8,128)(2,1)}, u32[]{:S(2)}) copy-start(bf16[192,1024]{1,0:T(8,128)(2,1)} %add_convert_fusion.1) | copy-start | bytes 1179652
  (7 other events, 23.4 us)
Sparse Core Ops, SparseCore 0:
  8.9 39.7 all-gather.8
  50.3 153.6 all-gather.6
  205.5 58.2 all-gather.10
  268.8 36.8 reduce-scatter.4
  307.7 35.8 all-gather.12
  363.9 38.3 reduce-scatter.6
  404.3 35.8 all-gather.14
  460.5 38.2 reduce-scatter.8
  500.9 35.8 all-gather.16
  557.4 38.3 reduce-scatter.10
where the time goes:
time: 605 us; the launch traced here: 604 us
  waiting for transfers between devices  475 us (79%)
  matrix products  61.7 us (10%)
  between operations  24.4 us (4%)
  local copies, waits for them, and re-layouts  19.6 us (3%)
  other arithmetic  16.7 us (3%)
  starting transfers between devices  7.09 us (1%)
    all_gather x1, waiting for transfers between devices, shards(): lax.all_gather(in_weights, 'ctx', axis=1, tiled=True)  153 us
    reduce_scatter x4, waiting for transfers between devices, combine(): lax.psum_scatter(partial_sum.astype(jnp.bfloat16), 'chan', scatter_dimens...  152 us
    all_gather x4, waiting for transfers between devices, expand_rows(): return lax.all_gather(hidden, 'chan', axis=1, tiled=True)  130 us
    all_gather x1, waiting for transfers between devices, shards(): lax.all_gather(out_weights, 'ctx', axis=1, tiled=True)  35.9 us
    dot_general x4, matrix products, stored_project(): jnp.dot(full_rows, chosen.reshape(chosen.shape[0], -1), preferred_element...  26.7 us
    conv_general_dilated x4, matrix products, causal_filter(): lax.conv_general_dilated(extended[None], filter_taps[::-1][:, None, :], (...  22.1 us
    dot_general x4, matrix products, stored_emit(): lax.dot_general(gated_bf, chosen, (((1,), (1,)), ((), ())), preferred_ele...  13 us
  transfers between devices with their start and end apart: 14, of which 13 were waited for; matrix products, arithmetic and copies ran while one was open for 5% of the time, Pallas kernels for 0%

commit v1 on v0

--- a/solution.py
+++ b/solution.py
@@ -3,6 +3,8 @@
 import jax
 import jax.numpy as jnp
 from jax import lax
+from jax.experimental import pallas as pl
+from jax.experimental.pallas import tpu as pltpu
 from jax.sharding import PartitionSpec as P
 
 STEPS = 4
@@ -106,18 +108,368 @@
     return hidden
 
 
+CHUNKS = 6
+PAD = 128
+LANES = 128
+BF = jnp.bfloat16
+F32 = jnp.float32
+
+
+def stationary_kernel(
+    sizes, plan, stream, w_in, w_out, taps, out,
+    h, p_send, p_recv, x_send, x_recv, own, ss_own, ss_recv, mixed, query, gat, acc, r_send, r_recv,
+    init_s, init_r, ss_s, ss_r, p_s, p_r, x_s, x_r, g_s, g_r, r_s, r_r, b_s, b_r, o_s, o_r, local_sem,
+):
+    tokens, rows, block, width, half = sizes
+    ctx, chan = lax.axis_index("ctx"), lax.axis_index("chan")
+    n_ctx, n_chan = 4, 4
+    side, core = ctx // 2, ctx % 2
+    partner = {"ctx": side * 2 + (1 - core)}
+    across = {"ctx": (1 - side) * 2 + core}
+    diagonal = {"ctx": (1 - side) * 2 + (1 - core)}
+    relations = (partner, across, diagonal)
+    last = n_chan - 1
+    place = (chan, last - chan)
+    onward = ({"chan": jnp.minimum(chan + 1, last)}, {"chan": jnp.maximum(chan - 1, 0)})
+    back = (onward[1], onward[0])
+
+    def remote(source, target, send, recv, device):
+        return pltpu.make_async_remote_copy(
+            src_ref=source, dst_ref=target, send_sem=send, recv_sem=recv,
+            device_id=device, device_id_type=pl.DeviceIdType.MESH,
+        )
+
+    barrier = pltpu.get_barrier_semaphore()
+    for di in range(n_ctx):
+        for dk in range(n_chan):
+            if di or dk:
+                pl.semaphore_signal(
+                    barrier, inc=1,
+                    device_id={"ctx": (ctx + di) % n_ctx, "chan": (chan + dk) % n_chan},
+                    device_id_type=pl.DeviceIdType.MESH,
+                )
+    pl.semaphore_wait(barrier, n_ctx * n_chan - 1)
+
+    block_rows = tokens // n_ctx
+    mine = pl.ds(pl.multiple_of(ctx * block_rows, block_rows), block_rows)
+
+    def init_copy(kappa):
+        return remote(stream, h.at[mine, :], init_s.at[kappa], init_r.at[ctx], {"ctx": chan, "chan": kappa})
+
+    def init_wait(source):
+        there = pl.ds(source * block_rows, block_rows)
+        return remote(stream, h.at[there, :], init_s.at[0], init_r.at[source], {"ctx": chan, "chan": 0})
+
+    corner = ctx == chan
+    for kappa in range(n_chan):
+        @pl.when(jnp.logical_not(corner & (chan == kappa)))
+        def _():
+            init_copy(kappa).start()
+
+    @pl.when(corner)
+    def _():
+        keep = pltpu.make_async_copy(stream, h.at[mine, :], local_sem)
+        keep.start()
+        keep.wait()
+
+    mixed[pl.ds(0, PAD), :] = jnp.zeros((PAD, LANES), F32)
+    for source in range(n_ctx):
+        @pl.when(jnp.logical_not(corner & (ctx == source)))
+        def _():
+            init_wait(source).wait_recv()
+    for kappa in range(n_chan):
+        @pl.when(jnp.logical_not(corner & (chan == kappa)))
+        def _():
+            init_copy(kappa).wait_send()
+
+    def span(t):
+        return pl.ds(pl.multiple_of(t * rows, rows), rows)
+
+    def ss_copy(rel, t):
+        return remote(ss_own.at[t], ss_recv.at[rel, t], ss_s.at[rel, t], ss_r.at[rel, t], relations[rel])
+
+    def p_copy(slot, t):
+        return remote(p_send.at[slot, t], p_recv.at[slot, t], p_s.at[slot, t], p_r.at[slot, t], partner)
+
+    def x_copy(t):
+        return remote(x_send.at[t], x_recv.at[t], x_s.at[t], x_r.at[t], across)
+
+    def lanes(index):
+        return pl.ds(pl.multiple_of(index * LANES, LANES), LANES)
+
+    def g_copy(kind, t, sending=True):
+        owner = (1 - side) * 2 + core if kind == 2 else ctx
+        if not sending:
+            owner = (across["ctx"], partner["ctx"], diagonal["ctx"])[kind]
+        ref = gat.at[span(t), lanes(owner)]
+        return remote(ref, ref, g_s.at[kind, t], g_r.at[kind, t], across if kind == 0 else partner)
+
+    def r_copy(d, t):
+        return remote(r_send.at[d, t], r_recv.at[d, t], r_s.at[d, t], r_r.at[d, t], onward[d])
+
+    def b_copy(d, t):
+        ref = h.at[span(t), pl.ds(d * half, half)]
+        return remote(ref, ref, b_s.at[d, t], b_r.at[d, t], back[d])
+
+    def take_back(t):
+        for d in range(2):
+            @pl.when(place[d] < last)
+            def _():
+                b_copy(d, t).wait_recv()
+
+            @pl.when((place[d] < last) & (place[d] > 0))
+            def _():
+                b_copy(d, t).start()
+
+    def each(count, body):
+        def wrapped(t, carry):
+            body(t)
+            return carry
+        lax.fori_loop(0, count, wrapped, 0)
+
+    def step(s, carry):
+        section = plan[s]
+
+        def project(t, index):
+            return jnp.dot(h[span(t), :], w_in[section, index], preferred_element_type=F32)
+
+        def enter(t):
+            @pl.when(s > 0)
+            def _():
+                take_back(t)
+
+            p_send[0, t] = project(t, diagonal["ctx"]).astype(BF)
+            p_copy(0, t).start()
+            wide = h[span(t), :].astype(F32)
+            squares = (wide * wide).astype(BF)
+            ss_own[t] = lax.dot_general(
+                jnp.ones((8, squares.shape[1]), BF), squares, (((1,), (1,)), ((), ())), preferred_element_type=F32
+            )
+            for rel in range(3):
+                ss_copy(rel, t).start()
+            passing = project(t, across["ctx"])
+            p_copy(0, t).wait_recv()
+            x_send[t] = (passing + p_recv[0, t].astype(F32)).astype(BF)
+            x_copy(t).start()
+            p_send[1, t] = project(t, partner["ctx"]).astype(BF)
+            p_copy(1, t).start()
+            own[t] = project(t, ctx)
+
+        each(CHUNKS, enter)
+
+        def mix(t):
+            for rel in range(3):
+                ss_copy(rel, t).wait_recv()
+            p_copy(1, t).wait_recv()
+            x_copy(t).wait_recv()
+            total = ss_own[t] + ss_recv[0, t] + ss_recv[1, t] + ss_recv[2, t]
+            scale = lax.rsqrt(total * (1.0 / width) + 1e-05)
+            scale = jnp.transpose(scale)[:, :1]
+            parts = (own[t] + p_recv[1, t].astype(F32) + x_recv[t].astype(F32)) * scale
+            query = parts[:, :LANES].astype(BF).astype(F32)
+            product = parts[:, LANES:2 * LANES] * parts[:, 2 * LANES:]
+            mixed[pl.ds(pl.multiple_of(PAD + t * rows, rows), rows), :] = product.astype(BF).astype(F32)
+
+            def tap_block(jj, total):
+                start = pl.multiple_of(PAD + t * rows - 8 * jj - 8, 8)
+                window = mixed[pl.ds(start, rows + 8), :]
+                weights = taps[section, jj]
+                for c in range(8):
+                    total = total + weights[c:c + 1, :] * window[8 - c:8 - c + rows, :]
+                return total
+
+            filtered = lax.fori_loop(0, taps.shape[1], tap_block, jnp.zeros((rows, LANES), F32))
+            gat[span(t), lanes(ctx)] = (query * filtered).astype(BF)
+            g_copy(0, t).start()
+            g_copy(1, t).start()
+
+        each(CHUNKS, mix)
+
+        def emit(t):
+            g_copy(0, t, False).wait_recv()
+            g_copy(2, t).start()
+            g_copy(1, t, False).wait_recv()
+
+        each(CHUNKS, emit)
+
+        def emit_dot(t):
+            g_copy(2, t, False).wait_recv()
+            gated = gat[span(t), :]
+            for d in range(2):
+                acc[d, t] = lax.dot_general(
+                    gated, w_out[section, d], (((1,), (1,)), ((), ())), preferred_element_type=F32
+                )
+
+                @pl.when(place[d] == 0)
+                def _():
+                    r_send[d, t] = acc[d, t].astype(BF)
+                    r_copy(d, t).start()
+
+            @pl.when(s > 0)
+            def _():
+                for d in range(2):
+                    @pl.when((place[d] < last) & (place[d] > 0))
+                    def _():
+                        b_copy(d, t).wait_send()
+
+                    @pl.when(place[d] == last)
+                    def _():
+                        b_copy(d, t).wait_send()
+
+        each(CHUNKS, emit_dot)
+
+        def chain(u):
+            for d in range(2):
+                t = u - (place[d] - 1)
+                inside = (t >= 0) & (t < CHUNKS)
+
+                @pl.when(inside & (place[d] > 0) & (place[d] < last))
+                def _():
+                    r_copy(d, t).wait_recv()
+                    r_send[d, t] = (acc[d, t] + r_recv[d, t].astype(F32)).astype(BF)
+                    r_copy(d, t).start()
+
+                @pl.when(inside & (place[d] == last))
+                def _():
+                    r_copy(d, t).wait_recv()
+                    update = acc[d, t] + r_recv[d, t].astype(F32)
+                    columns = pl.ds(d * half, half)
+                    h[span(t), columns] = (h[span(t), columns].astype(F32) + update).astype(BF)
+                    b_copy(d, t).start()
+
+        each(CHUNKS + last - 1, chain)
+
+        def settle(t):
+            for slot in range(2):
+                p_copy(slot, t).wait_send()
+            for rel in range(3):
+                ss_copy(rel, t).wait_send()
+            x_copy(t).wait_send()
+            for kind in range(3):
+                g_copy(kind, t).wait_send()
+            for d in range(2):
+                @pl.when(place[d] < last)
+                def _():
+                    r_copy(d, t).wait_send()
+
+        each(CHUNKS, settle)
+        return carry
+
+    lax.fori_loop(0, STEPS, step, 0)
+    each(CHUNKS, take_back)
+
+    def finish(t):
+        for d in range(2):
+            @pl.when(place[d] > 0)
+            def _():
+                b_copy(d, t).wait_send()
+
+    each(CHUNKS, finish)
+
+    def out_copy(target):
+        there = pl.ds(target * block_rows, block_rows)
+        return remote(h.at[there, :], out, o_s.at[target], o_r, {"ctx": target})
+
+    @pl.when(corner)
+    def _():
+        for target in range(n_ctx):
+            @pl.when(ctx != target)
+            def _():
+                out_copy(target).start()
+        keep = pltpu.make_async_copy(h.at[mine, :], out, local_sem)
+        keep.start()
+        keep.wait()
+        for target in range(n_ctx):
+            @pl.when(ctx != target)
+            def _():
+                out_copy(target).wait_send()
+
+    @pl.when(jnp.logical_not(corner))
+    def _():
+        out_copy(0).wait_recv()
+
+
+def stationary(stream, in_weights, out_weights, short_taps, medium_taps, plan):
+    n_ctx = lax.axis_size("ctx")
+    n_chan = lax.axis_size("chan")
+    ctx = lax.axis_index("ctx")
+    features, channels = in_weights.shape[1], in_weights.shape[3]
+    tokens = stream.shape[0] * n_ctx
+    rows = tokens // CHUNKS
+    half = features // 2
+    block = 3 * LANES
+    reach = medium_taps.shape[0]
+    w_in = in_weights.reshape(2, features, 3, n_ctx, LANES).transpose(0, 3, 1, 2, 4).reshape(2, n_ctx, features, block)
+    w_out = out_weights.reshape(2, 2, half, channels)
+    taps = jnp.stack([section_taps(section, short_taps, medium_taps) for section in range(2)])
+    taps = lax.dynamic_slice_in_dim(taps, ctx * LANES, LANES, 2).astype(F32)
+    taps = taps.reshape(2, reach // 8, 8, LANES)
+    vmem = pl.BlockSpec(memory_space=pltpu.VMEM)
+    dma = pltpu.SemaphoreType.DMA
+    scratch = [
+        pltpu.VMEM((tokens, features), BF),
+        pltpu.VMEM((2, CHUNKS, rows, block), BF),
+        pltpu.VMEM((2, CHUNKS, rows, block), BF),
+        pltpu.VMEM((CHUNKS, rows, block), BF),
+        pltpu.VMEM((CHUNKS, rows, block), BF),
+        pltpu.VMEM((CHUNKS, rows, block), F32),
+        pltpu.VMEM((CHUNKS, 8, rows), F32),
+        pltpu.VMEM((3, CHUNKS, 8, rows), F32),
+        pltpu.VMEM((PAD + tokens, LANES), F32),
+        pltpu.VMEM((8, LANES), F32),
+        pltpu.VMEM((tokens, channels), BF),
+        pltpu.VMEM((2, CHUNKS, rows, half), F32),
+        pltpu.VMEM((2, CHUNKS, rows, half), BF),
+        pltpu.VMEM((2, CHUNKS, rows, half), BF),
+        dma((n_chan,)), dma((n_ctx,)),
+        dma((3, CHUNKS)), dma((3, CHUNKS)),
+        dma((2, CHUNKS)), dma((2, CHUNKS)),
+        dma((CHUNKS,)), dma((CHUNKS,)),
+        dma((3, CHUNKS)), dma((3, CHUNKS)),
+        dma((2, CHUNKS)), dma((2, CHUNKS)),
+        dma((2, CHUNKS)), dma((2, CHUNKS)),
+        dma((n_ctx,)), dma(()), dma(()),
+    ]
+    sizes = (tokens, rows, block, features * n_ctx, half)
+    return pl.pallas_call(
+        partial(stationary_kernel, sizes),
+        out_shape=jax.ShapeDtypeStruct(stream.shape, stream.dtype),
+        in_specs=[pl.BlockSpec(memory_space=pltpu.SMEM)] + [vmem] * 4,
+        out_specs=vmem,
+        scratch_shapes=scratch,
+        compiler_params=pltpu.CompilerParams(
+            collective_id=0, has_side_effects=True, vmem_limit_bytes=60 * 1024 * 1024
+        ),
+    )(plan, stream, w_in, w_out, taps)
+
+
+def fits(mesh, stream, in_weights, medium_taps):
+    n_ctx, n_chan = mesh.shape["ctx"], mesh.shape["chan"]
+    tokens = stream.shape[0] // mesh.shape["groups"]
+    channels = in_weights.shape[3] // n_chan
+    return (
+        n_ctx == 4 and n_chan == 4 and channels == n_ctx * LANES
+        and stream.shape[1] // n_chan == in_weights.shape[1] // n_ctx
+        and tokens % (CHUNKS * PAD) == 0 and medium_taps.shape[0] <= PAD and tokens // CHUNKS == PAD
+    )
+
+
 def solution(mesh):
-    return jax.shard_map(
-        shards,
-        mesh=mesh,
-        in_specs=(
-            P(("groups", "ctx"), "chan"),
-            P(None, "ctx", None, "chan"),
-            P(None, "ctx", "chan"),
-            P(None, "chan"),
-            P(None, "chan"),
-            P(),
-        ),
-        out_specs=P(("groups", "ctx"), "chan"),
-        check_vma=False,
-    )
+    def run(stream, in_weights, out_weights, short_taps, medium_taps, plan):
+        body = stationary if fits(mesh, stream, in_weights, medium_taps) else shards
+        return jax.shard_map(
+            body,
+            mesh=mesh,
+            in_specs=(
+                P(("groups", "ctx"), "chan"),
+                P(None, "ctx", None, "chan"),
+                P(None, "ctx", "chan"),
+                P(None, "chan"),
+                P(None, "chan"),
+                P(),
+            ),
+            out_specs=P(("groups", "ctx"), "chan"),
+            check_vma=False,
+        )(stream, in_weights, out_weights, short_taps, medium_taps, plan)
+
+    return run

time: 605 us -> 515 us (0.85)
  Pallas kernels: 0 us -> 487 us
  waiting for transfers between devices: 475 us -> 0 us
  matrix products: 61.7 us -> 0 us
  between operations: 24.4 us -> 0.05 us
  other arithmetic: 16.7 us -> 0.02 us
  starting transfers between devices: 7.09 us -> 0 us
  local copies, waits for them, and re-layouts: 19.6 us -> 26.6 us
    pallas_call x0 -> x1, Pallas kernels: none -> 487 us  [stationary(): pl.pallas_call(partial(stationary_kernel, sizes), out_shape=jax.ShapeDtyp...]
    all_gather x6 -> x0, waiting for transfers between devices: 319 us -> none  [the longest x1 153 us: shards(): lax.all_gather(in_weights, 'ctx', axis=1, tiled=True)]
    reduce_scatter x4 -> x0, waiting for transfers between devices: 152 us -> none  [combine(): lax.psum_scatter(partial_sum.astype(jnp.bfloat16), 'chan', scatter_dimens...]
    dot_general x8 -> x0, matrix products: 39.7 us -> none  [the longest x4 26.7 us: stored_project(): jnp.dot(full_rows, chosen.reshape(chosen.shape[0], -1), preferred_element...]
    conv_general_dilated x4 -> x0, matrix products: 22.1 us -> none  [causal_filter(): lax.conv_general_dilated(extended[None], filter_taps[::-1][:, None, :], (...]
    reshape x1 -> x2, local copies, waits for them, and re-layouts: 0.9 us -> 9.42 us  [the longest x1 8.66 us: stationary(): in_weights.reshape(2, features, 3, n_ctx, LANES).transpose(0, 3, 1, 2, 4)]
    convert_element_type x11 -> x0, other arithmetic: 8.45 us -> none  [the longest x4 7.51 us: combine(): return (hidden.astype(jnp.float32) + update).astype(jnp.bfloat16)]
    reduce_sum x4 -> x0, other arithmetic: 7.56 us -> none  [advance(): jnp.mean(widened * widened, axis=1, keepdims=True) + 1e-05]
  transfers between devices with their start and end apart: 14 -> 0, of which waited for: 13 -> 0; matrix products, arithmetic and copies ran while one was open for 5% -> 0% of each run, Pallas kernels for 0% -> 0%
where the time goes in v1:
time: 515 us; the launch traced here: 513 us
  Pallas kernels  487 us (95%)
  local copies, waits for them, and re-layouts  26.6 us (5%)
    pallas_call x1, Pallas kernels, stationary(): pl.pallas_call(partial(stationary_kernel, sizes), out_shape=jax.ShapeDtyp...  487 us
    unnamed x7, local copies, waits for them, and re-layouts  10.6 us

profile of v1, /device:TPU:0, one launch (start us, length us, event | category | flops | bytes accessed | tf_op | source)
XLA Modules:
  0.0 513.3 jit_solution(3438284125108997517)
XLA Ops:
  0.0 8.6 %copy.12 = bf16[2,1024,3,512]{1,3,2,0:T(8,128)(2,1)} copy(bf16[2,1024,3,512]{3,1,2,0:T(8,128)(2,1)} %param.7) | data formatting | bytes 12582912 | tf_op args[1]
  8.6 6.5 %copy.13 = bf16[2,4,1024,3,128]{2,4,3,1,0:T(8,128)(2,1)} copy(bf16[2,4,1024,3,128]{2,4,1,3,0:T(8,128)(2,1)} %bitcast.10) | data formatting | bytes 12582912 | tf_op jit(solution)/shard_map/transpose | solution.py:402
  15.2 0.0 copy-start
  15.2 0.0 copy-start.1
  15.2 8.7 %copy.16.w_in = bf16[2,4,1024,384]{3,2,1,0:T(8,128)(2,1)} copy(bf16[2,4,1024,384]{2,3,1,0:T(8,128)(2,1)} %bitcast.9) | data formatting | bytes 12582912 | tf_op jit(solution)/shard_map/reshape | solution.py:402
  23.8 0.0 copy-done
  23.8 0.2 copy.14
  24.0 0.0 copy-done.1
  24.1 0.8 copy.15
  24.9 486.6 %shard_map.64 = bf16[192,1024]{1,0:T(8,128)(2,1)} custom-call(s32[4]{0:T(128)} %plan.1, bf16[192,1024]{1,0:T(8,128)(2,1)} %stream.1, bf16[2,4,1024,384]{3,2,1,0:T(8,128)(2,1)} %copy.16.w_in, bf16[2,2,512,512]{3,2,1,0:T(8,128)(2,1)} %bitcast.11, f32[2,16,8,128]{3,2,1,0:T(8,128)} %bitcast.12), custom_call_target="tpu_custom_call" | custom-call | tf_op jit(solution)/shard_map/pallas_call | solution.py:434
  511.5 1.8 copy.18
  (3 shorter events, 0.1 us)
Async XLA Ops:
  15.2 8.7 %copy-start = (bf16[7,512]{1,0:T(8,128)(2,1)S(1)}, bf16[7,512]{1,0:T(8,128)(2,1)}, u32[]{:S(2)}) copy-start(bf16[7,512]{1,0:T(8,128)(2,1)} %param.9) | copy-start | bytes 21508
  15.2 8.9 %copy-start.1 = (bf16[128,32]{0,1:T(8,128)(2,1)S(1)}, bf16[128,32]{0,1:T(8,128)(2,1)}, u32[]{:S(2)}) copy-start(bf16[128,32]{0,1:T(8,128)(2,1)} %param.10) | copy-start | bytes 24580

commit v2 on v1

--- a/solution.py
+++ b/solution.py
@@ -109,6 +109,7 @@
 
 
 CHUNKS = 6
+SKEW = 2
 PAD = 128
 LANES = 128
 BF = jnp.bfloat16
@@ -211,15 +212,11 @@
         ref = h.at[span(t), pl.ds(d * half, half)]
         return remote(ref, ref, b_s.at[d, t], b_r.at[d, t], back[d])
 
-    def take_back(t):
+    def arrive(t):
         for d in range(2):
-            @pl.when(place[d] < last)
+            @pl.when(place[d] == 0)
             def _():
                 b_copy(d, t).wait_recv()
-
-            @pl.when((place[d] < last) & (place[d] > 0))
-            def _():
-                b_copy(d, t).start()
 
     def each(count, body):
         def wrapped(t, carry):
@@ -231,15 +228,15 @@
         section = plan[s]
 
         def project(t, index):
-            return jnp.dot(h[span(t), :], w_in[section, index], preferred_element_type=F32)
+            columns = lanes(index)
+            weights = jnp.concatenate([w_in[section, j, :, columns] for j in range(3)], 1)
+            return jnp.dot(h[span(t), :], weights, preferred_element_type=F32)
 
         def enter(t):
-            @pl.when(s > 0)
-            def _():
-                take_back(t)
-
             p_send[0, t] = project(t, diagonal["ctx"]).astype(BF)
             p_copy(0, t).start()
+            p_send[1, t] = project(t, partner["ctx"]).astype(BF)
+            p_copy(1, t).start()
             wide = h[span(t), :].astype(F32)
             squares = (wide * wide).astype(BF)
             ss_own[t] = lax.dot_general(
@@ -247,15 +244,28 @@
             )
             for rel in range(3):
                 ss_copy(rel, t).start()
+
+        def cross(t):
             passing = project(t, across["ctx"])
             p_copy(0, t).wait_recv()
             x_send[t] = (passing + p_recv[0, t].astype(F32)).astype(BF)
             x_copy(t).start()
-            p_send[1, t] = project(t, partner["ctx"]).astype(BF)
-            p_copy(1, t).start()
             own[t] = project(t, ctx)
 
-        each(CHUNKS, enter)
+        def entering(u):
+            @pl.when(u < CHUNKS)
+            def _():
+                @pl.when(s > 0)
+                def _():
+                    arrive(u)
+
+                enter(u)
+
+            @pl.when(u > 0)
+            def _():
+                cross(u - 1)
+
+        each(CHUNKS + 1, entering)
 
         def mix(t):
             for rel in range(3):
@@ -320,7 +330,7 @@
 
         def chain(u):
             for d in range(2):
-                t = u - (place[d] - 1)
+                t = u - (place[d] - 1) * SKEW
                 inside = (t >= 0) & (t < CHUNKS)
 
                 @pl.when(inside & (place[d] > 0) & (place[d] < last))
@@ -337,7 +347,16 @@
                     h[span(t), columns] = (h[span(t), columns].astype(F32) + update).astype(BF)
                     b_copy(d, t).start()
 
-        each(CHUNKS + last - 1, chain)
+            for d in range(2):
+                t = u - (2 + last - place[d]) * SKEW
+                inside = (t >= 0) & (t < CHUNKS)
+
+                @pl.when(inside & (place[d] > 0) & (place[d] < last))
+                def _():
+                    b_copy(d, t).wait_recv()
+                    b_copy(d, t).start()
+
+        each(CHUNKS + (2 * last - 2) * SKEW, chain)
 
         def settle(t):
             for slot in range(2):
@@ -356,7 +375,7 @@
         return carry
 
     lax.fori_loop(0, STEPS, step, 0)
-    each(CHUNKS, take_back)
+    each(CHUNKS, arrive)
 
     def finish(t):
         for d in range(2):
@@ -399,7 +418,7 @@
     half = features // 2
     block = 3 * LANES
     reach = medium_taps.shape[0]
-    w_in = in_weights.reshape(2, features, 3, n_ctx, LANES).transpose(0, 3, 1, 2, 4).reshape(2, n_ctx, features, block)
+    w_in = in_weights.transpose(0, 2, 1, 3)
     w_out = out_weights.reshape(2, 2, half, channels)
     taps = jnp.stack([section_taps(section, short_taps, medium_taps) for section in range(2)])
     taps = lax.dynamic_slice_in_dim(taps, ctx * LANES, LANES, 2).astype(F32)
@@ -450,7 +469,7 @@
     return (
         n_ctx == 4 and n_chan == 4 and channels == n_ctx * LANES
         and stream.shape[1] // n_chan == in_weights.shape[1] // n_ctx
-        and tokens % (CHUNKS * PAD) == 0 and medium_taps.shape[0] <= PAD and tokens // CHUNKS == PAD
+        and tokens % (CHUNKS * PAD) == 0 and medium_taps.shape[0] <= PAD
     )
 
 

time: 515 us -> 310 us (0.60)
  Pallas kernels: 487 us -> 305 us
  local copies, waits for them, and re-layouts: 26.6 us -> 4.14 us
    pallas_call x1, Pallas kernels: 487 us -> 305 us  [stationary(): pl.pallas_call(partial(stationary_kernel, sizes), out_shape=jax.ShapeDtyp...]
    reshape x1 -> x0, local copies, waits for them, and re-layouts: 8.66 us -> none  [stationary(): in_weights.reshape(2, features, 3, n_ctx, LANES).transpose(0, 3, 1, 2, 4)]
    unnamed x7 -> x2, local copies, waits for them, and re-layouts: 10.6 us -> 2.64 us
    transpose x1 -> x0, local copies, waits for them, and re-layouts: 6.51 us -> none  [stationary(): in_weights.reshape(2, features, 3, n_ctx, LANES).transpose(0, 3, 1, 2, 4)]
where the time goes in v2:
time: 310 us
  Pallas kernels  305 us (98%)
  local copies, waits for them, and re-layouts  4.14 us (1%)
    pallas_call x1, Pallas kernels, stationary(): pl.pallas_call(partial(stationary_kernel, sizes), out_shape=jax.ShapeDtyp...  305 us

profile of v2, /device:TPU:0, one launch (start us, length us, event | category | flops | bytes accessed | tf_op | source)
XLA Modules:
  0.0 309.5 jit_solution(2551653306243715105)
XLA Ops:
  0.0 0.9 copy.8
  0.9 0.7 broadcast_in_dim.2
  1.7 0.8 copy.9
  2.4 305.4 %shard_map.64 = bf16[192,1024]{1,0:T(8,128)(2,1)} custom-call(s32[4]{0:T(128)} %plan.1, bf16[192,1024]{1,0:T(8,128)(2,1)} %stream.1, bf16[2,3,1024,512]{3,2,1,0:T(8,128)(2,1)} %bitcast.6, bf16[2,2,512,512]{3,2,1,0:T(8,128)(2,1)} %bitcast.7, f32[2,16,8,128]{3,2,1,0:T(8,128)} %bitcast.8), custom_call_target="tpu_custom_call" | custom-call | tf_op jit(solution)/shard_map/pallas_call | solution.py:453
  307.8 1.8 copy.11
  (2 shorter events, 0.0 us)

commit v3 on v2

--- a/solution.py
+++ b/solution.py
@@ -110,6 +110,7 @@
 
 CHUNKS = 6
 SKEW = 2
+ENTRY = 9
 PAD = 128
 LANES = 128
 BF = jnp.bfloat16
@@ -224,48 +225,48 @@
             return carry
         lax.fori_loop(0, count, wrapped, 0)
 
+    def project(section, t, index):
+        columns = lanes(index)
+        weights = jnp.concatenate([w_in[section, j, :, columns] for j in range(3)], 1)
+        return jnp.dot(h[span(t), :], weights, preferred_element_type=F32)
+
+    def enter(section, t):
+        p_send[0, t] = project(section, t, diagonal["ctx"]).astype(BF)
+        p_copy(0, t).start()
+        p_send[1, t] = project(section, t, partner["ctx"]).astype(BF)
+        p_copy(1, t).start()
+        wide = h[span(t), :].astype(F32)
+        squares = (wide * wide).astype(BF)
+        ss_own[t] = lax.dot_general(
+            jnp.ones((8, squares.shape[1]), BF), squares, (((1,), (1,)), ((), ())), preferred_element_type=F32
+        )
+        for rel in range(3):
+            ss_copy(rel, t).start()
+
+    def cross(section, t):
+        passing = project(section, t, across["ctx"])
+        p_copy(0, t).wait_recv()
+        x_send[t] = (passing + p_recv[0, t].astype(F32)).astype(BF)
+        x_copy(t).start()
+        own[t] = project(section, t, ctx)
+
+    def entering(s, u):
+        section = plan[s]
+
+        @pl.when((u >= 0) & (u < CHUNKS))
+        def _():
+            @pl.when(s > 0)
+            def _():
+                arrive(u)
+
+            enter(section, u)
+
+        @pl.when((u > 0) & (u <= CHUNKS))
+        def _():
+            cross(section, u - 1)
+
     def step(s, carry):
         section = plan[s]
-
-        def project(t, index):
-            columns = lanes(index)
-            weights = jnp.concatenate([w_in[section, j, :, columns] for j in range(3)], 1)
-            return jnp.dot(h[span(t), :], weights, preferred_element_type=F32)
-
-        def enter(t):
-            p_send[0, t] = project(t, diagonal["ctx"]).astype(BF)
-            p_copy(0, t).start()
-            p_send[1, t] = project(t, partner["ctx"]).astype(BF)
-            p_copy(1, t).start()
-            wide = h[span(t), :].astype(F32)
-            squares = (wide * wide).astype(BF)
-            ss_own[t] = lax.dot_general(
-                jnp.ones((8, squares.shape[1]), BF), squares, (((1,), (1,)), ((), ())), preferred_element_type=F32
-            )
-            for rel in range(3):
-                ss_copy(rel, t).start()
-
-        def cross(t):
-            passing = project(t, across["ctx"])
-            p_copy(0, t).wait_recv()
-            x_send[t] = (passing + p_recv[0, t].astype(F32)).astype(BF)
-            x_copy(t).start()
-            own[t] = project(t, ctx)
-
-        def entering(u):
-            @pl.when(u < CHUNKS)
-            def _():
-                @pl.when(s > 0)
-                def _():
-                    arrive(u)
-
-                enter(u)
-
-            @pl.when(u > 0)
-            def _():
-                cross(u - 1)
-
-        each(CHUNKS + 1, entering)
 
         def mix(t):
             for rel in range(3):
@@ -293,14 +294,10 @@
             g_copy(0, t).start()
             g_copy(1, t).start()
 
-        each(CHUNKS, mix)
-
         def emit(t):
             g_copy(0, t, False).wait_recv()
             g_copy(2, t).start()
             g_copy(1, t, False).wait_recv()
-
-        each(CHUNKS, emit)
 
         def emit_dot(t):
             g_copy(2, t, False).wait_recv()
@@ -326,37 +323,13 @@
                     def _():
                         b_copy(d, t).wait_send()
 
-        each(CHUNKS, emit_dot)
-
-        def chain(u):
-            for d in range(2):
-                t = u - (place[d] - 1) * SKEW
-                inside = (t >= 0) & (t < CHUNKS)
-
-                @pl.when(inside & (place[d] > 0) & (place[d] < last))
+        def filtering(u):
+            for lag, body in ((0, mix), (2, emit), (4, emit_dot)):
+                @pl.when((u >= lag) & (u < CHUNKS + lag))
                 def _():
-                    r_copy(d, t).wait_recv()
-                    r_send[d, t] = (acc[d, t] + r_recv[d, t].astype(F32)).astype(BF)
-                    r_copy(d, t).start()
-
-                @pl.when(inside & (place[d] == last))
-                def _():
-                    r_copy(d, t).wait_recv()
-                    update = acc[d, t] + r_recv[d, t].astype(F32)
-                    columns = pl.ds(d * half, half)
-                    h[span(t), columns] = (h[span(t), columns].astype(F32) + update).astype(BF)
-                    b_copy(d, t).start()
-
-            for d in range(2):
-                t = u - (2 + last - place[d]) * SKEW
-                inside = (t >= 0) & (t < CHUNKS)
-
-                @pl.when(inside & (place[d] > 0) & (place[d] < last))
-                def _():
-                    b_copy(d, t).wait_recv()
-                    b_copy(d, t).start()
-
-        each(CHUNKS + (2 * last - 2) * SKEW, chain)
+                    body(u - lag)
+
+        each(CHUNKS + 4, filtering)
 
         def settle(t):
             for slot in range(2):
@@ -366,14 +339,54 @@
             x_copy(t).wait_send()
             for kind in range(3):
                 g_copy(kind, t).wait_send()
+
+        each(CHUNKS, settle)
+
+        def chain(u):
+            for d in range(2):
+                t = u - (place[d] - 1) * SKEW
+                inside = (t >= 0) & (t < CHUNKS)
+
+                @pl.when(inside & (place[d] > 0) & (place[d] < last))
+                def _():
+                    r_copy(d, t).wait_recv()
+                    r_send[d, t] = (acc[d, t] + r_recv[d, t].astype(F32)).astype(BF)
+                    r_copy(d, t).start()
+
+                @pl.when(inside & (place[d] == last))
+                def _():
+                    r_copy(d, t).wait_recv()
+                    update = acc[d, t] + r_recv[d, t].astype(F32)
+                    columns = pl.ds(d * half, half)
+                    h[span(t), columns] = (h[span(t), columns].astype(F32) + update).astype(BF)
+                    b_copy(d, t).start()
+
+            for d in range(2):
+                t = u - (2 + last - place[d]) * SKEW
+                inside = (t >= 0) & (t < CHUNKS)
+
+                @pl.when(inside & (place[d] > 0) & (place[d] < last))
+                def _():
+                    b_copy(d, t).wait_recv()
+                    b_copy(d, t).start()
+
+            @pl.when(s + 1 < STEPS)
+            def _():
+                entering(s + 1, u - ENTRY)
+
+        each(jnp.where(s + 1 < STEPS, CHUNKS + 1 + ENTRY, CHUNKS + (2 * last - 2) * SKEW), chain)
+
+
+        def settle_chain(t):
             for d in range(2):
                 @pl.when(place[d] < last)
                 def _():
                     r_copy(d, t).wait_send()
 
-        each(CHUNKS, settle)
+        each(CHUNKS, settle_chain)
         return carry
 
+    each(CHUNKS + 1, partial(entering, 0))
     lax.fori_loop(0, STEPS, step, 0)
     each(CHUNKS, arrive)
 

time: 310 us -> 300 us (0.968)
  Pallas kernels: 305 us -> 296 us
    pallas_call x1, Pallas kernels: 305 us -> 296 us  [stationary(): pl.pallas_call(partial(stationary_kernel, sizes), out_shape=jax.ShapeDtyp...]
where the time goes in v3:
time: 300 us
  Pallas kernels  296 us (99%)
  local copies, waits for them, and re-layouts  4.14 us (1%)
    pallas_call x1, Pallas kernels, stationary(): pl.pallas_call(partial(stationary_kernel, sizes), out_shape=jax.ShapeDtyp...  296 us

profile of v3, /device:TPU:0, one launch (start us, length us, event | category | flops | bytes accessed | tf_op | source)
XLA Modules:
  0.0 299.8 jit_solution(7221047278002312992)
XLA Ops:
  0.0 0.9 copy.8
  0.9 0.7 broadcast_in_dim.2
  1.7 0.8 copy.9
  2.4 295.6 %shard_map.64 = bf16[192,1024]{1,0:T(8,128)(2,1)} custom-call(s32[4]{0:T(128)} %plan.1, bf16[192,1024]{1,0:T(8,128)(2,1)} %stream.1, bf16[2,3,1024,512]{3,2,1,0:T(8,128)(2,1)} %bitcast.6, bf16[2,2,512,512]{3,2,1,0:T(8,128)(2,1)} %bitcast.7, f32[2,16,8,128]{3,2,1,0:T(8,128)} %bitcast.8), custom_call_target="tpu_custom_call" | custom-call | tf_op jit(solution)/shard_map/pallas_call | solution.py:466
  298.0 1.8 copy.11
  (2 shorter events, 0.1 us)
